TPU v7x, 32 devices: a whole 2x2x4 slice. The times are simulated.
32 devices in a mesh: space: 2 (over y), chaos: 16 (over z, x, core).
Axes of the slice: x: 2, y: 2, z: 4, core: 2. Of those that a mesh axis runs over, the one named last changes fastest.
Arguments:
- kl_fields: float32 [9, 4, 16, 512], P(None, None, 'space'), may hold values from -5 to 5
- labels: int32 [4, 16, 512], P(None, 'space'), may hold values from 0 to 3
- region_scale: float32 [4, 9], replicated, may hold values from 0.5 to 2
- background: float32 [4, 16, 512], P(None, 'space'), may hold values from -4 to 4
- galerkin_table: int32 [384, 3], replicated, may hold values from 0 to 47, as said below
- triple_values: float32 [384], replicated, may hold values from -4 to 4
- direction: float32 [48, 3, 4, 16, 512], P('chaos', None, None, 'space'), may hold values from -6 to 6
Outputs:
- result: float32 [48, 3, 4, 16, 512], P('chaos', None, None, 'space')
Inputs may be any that keep to these rules, and one draw needn't show every extreme that they name: `galerkin_table`: row r has term i = r // 8; the first row of each term is (i, i, 0); the others name any term j and a mode k of 1 to 8.
All inputs are finite; a program needn't handle non-finite values.
Results may differ from a plain program's by a relative error of at most 0.000076.
Values sent between devices are 32-bit elements; how exact they have to be, the bound alone decides.
A program may use at most 128 MiB of HBM per device.

v0:
```python
import jax
import jax.numpy as jnp
from jax import lax
from jax.sharding import PartitionSpec as P


def extended(array, sides, width):
    for axis, dim in sides:
        size, length = (lax.axis_size(axis), array.shape[dim])
        up = [(i, (i + 1) % size) for i in range(size - 1)]
        down = [(j, i) for i, j in up]
        last = lax.slice_in_dim(array, length - width, length, axis=dim)
        initial = lax.slice_in_dim(array, 0, width, axis=dim)
        before = lax.ppermute(last, axis, up)
        after = lax.ppermute(initial, axis, down)
        array = jnp.concatenate([before, array, after], axis=dim)
    return array


def neighbours(padded):
    middle = padded[..., 1:-1, :]
    row_next = padded[..., 2:, :]
    row_prev = padded[..., :-2, :]
    plane_zero = jnp.zeros_like(middle[..., :1, :, :])
    plane_next = jnp.concatenate([middle[..., 1:, :, :], plane_zero], axis=-3)
    plane_prev = jnp.concatenate([plane_zero, middle[..., :-1, :, :]], axis=-3)
    column_zero = jnp.zeros_like(middle[..., :1])
    column_next = jnp.concatenate([middle[..., 1:], column_zero], axis=-1)
    column_prev = jnp.concatenate([column_zero, middle[..., :-1]], axis=-1)
    return (middle, (row_next, row_prev, plane_next, plane_prev, column_next, column_prev))


def drift_terms(potential_pad):
    middle, beside_all = neighbours(potential_pad)
    return tuple((0.5 * (other - middle) for other in beside_all))


def jacobian_block(coef_pad, potential_pad, electron_pad, hole_pad, drift_list):
    coef_mid, coef_nbr = neighbours(coef_pad)
    pot_mid, pot_nbr = neighbours(potential_pad)
    ele_mid, ele_nbr = neighbours(electron_pad)
    hole_mid, hole_nbr = neighbours(hole_pad)
    out_potential = coef_mid * (ele_mid - hole_mid)
    out_electron = jnp.zeros_like(out_potential)
    out_holes = jnp.zeros_like(out_potential)
    for facing in range(6):
        conduct = 0.5 * (coef_mid + coef_nbr[facing])
        potential_rise = pot_nbr[facing] - pot_mid
        drift_now = drift_list[facing]
        out_potential = out_potential - conduct * potential_rise
        out_electron = out_electron + conduct * (
            ele_mid - ele_nbr[facing] - drift_now * (ele_mid + ele_nbr[facing]) - potential_rise
        )
        out_holes = out_holes + conduct * (
            hole_mid - hole_nbr[facing] + drift_now * (hole_mid + hole_nbr[facing]) + potential_rise
        )
    return jnp.stack([out_potential, out_electron, out_holes], axis=-4)


def shards(kl_fields, labels, region_scale, background, galerkin_table, triple_values, direction):
    term_dev = direction.shape[0]
    group_count = lax.axis_size("chaos")
    all_terms = term_dev * group_count
    first_term = lax.axis_index("chaos") * term_dev
    region_count = region_scale.shape[0]
    mode_count = region_scale.shape[1]
    lookup = jnp.zeros(kl_fields.shape, jnp.float32)
    for region in range(region_count):
        lookup = (
            lookup
            + (labels == region).astype(jnp.float32)[None]
            * region_scale[region][:, None, None, None]
        )
    scaled = kl_fields * lookup
    stacked = jnp.concatenate([scaled, background[None]], axis=0)
    rimmed = extended(stacked, (("space", 2),), 1)
    coef_pad = rimmed[:-1]
    drift_list = drift_terms(rimmed[-1])
    local_hot = (
        galerkin_table[:, 0][:, None] == first_term + jnp.arange(term_dev, dtype=jnp.int32)[None]
    ).astype(jnp.float32)
    source_hot = (
        galerkin_table[:, 1][:, None] == jnp.arange(all_terms, dtype=jnp.int32)[None]
    ).astype(jnp.float32)
    mode_hot = (
        galerkin_table[:, 2][:, None] == jnp.arange(mode_count, dtype=jnp.int32)[None]
    ).astype(jnp.float32)
    mixing = jnp.einsum(
        "t,ta,tj,tk->ajk",
        triple_values,
        local_hot,
        source_hot,
        mode_hot,
        precision=lax.Precision.HIGHEST,
    )
    zeros_out = jnp.zeros(direction.shape, jnp.float32)
    own_pad = extended(direction, (("space", 3),), 1)
    term_block = lax.all_gather(own_pad, "chaos", axis=0, tiled=True)
    block_terms = term_block.shape[0]

    def one_pair(pair_index, total):
        target = pair_index // block_terms
        source = pair_index % block_terms
        pair_weights = mixing[target, source]

        def apply_pair(unused):
            pair_coef = jnp.einsum(
                "k,kprc->prc", pair_weights, coef_pad, precision=lax.Precision.HIGHEST
            )
            fields = lax.dynamic_index_in_dim(term_block, source, 0, keepdims=False)
            return jacobian_block(pair_coef, fields[0], fields[1], fields[2], drift_list)

        def skip_pair(unused):
            return jnp.zeros(direction.shape[1:], jnp.float32)

        update = lax.cond(jnp.any(pair_weights != 0.0), apply_pair, skip_pair, 0)
        current = lax.dynamic_index_in_dim(total, target, 0, keepdims=False)
        return lax.dynamic_update_index_in_dim(total, current + update, target, 0)

    return lax.fori_loop(0, term_dev * block_terms, one_pair, zeros_out)


def solution(mesh):
    return jax.shard_map(
        shards,
        mesh=mesh,
        in_specs=(
            P(None, None, "space", None),
            P(None, "space", None),
            P(),
            P(None, "space", None),
            P(),
            P(),
            P("chaos", None, None, "space", None),
        ),
        out_specs=P("chaos", None, None, "space", None),
        check_vma=False,
    )
```

profile of v0, /device:TPU:0, one launch (start us, length us, event | category | flops | bytes accessed | tf_op | source)
XLA Modules:
  0.0 422.6 jit_solution(8876589187335992419)
XLA Ops:
  8.0 5.0 %collective-permute-start.2 = (f32[3,3,4,1,512]{4,2,3,1,0:T(4,128)S(1)}, f32[3,3,4,1,512]{4,2,3,1,0:T(4,128)S(1)}, u32[]{:S(2)}, u32[]{:S(2)}) collective-permute-start(f32[3,3,4,1,512]{4,2,3,1,0:T(4,128)S(1)} %get-tuple-element.391), channel_id=1, source_target_pairs={{0,16},{1,17},{2,18},{3,19},{4,20},{5,21},{6,22},{7,23},{8,24},{9,... | collective-permute-start | bytes 221192 | tf_op jit(solution)/shard_map/ppermute | solution.py:14
  15.0 4.3 %collective-permute-done.3 = f32[3,3,4,1,512]{4,2,3,1,0:T(4,128)S(1)} collective-permute-done((f32[3,3,4,1,512]{4,2,3,1,0:T(4,128)S(1)}, f32[3,3,4,1,512]{4,2,3,1,0:T(4,128)S(1)}, u32[]{:S(2)}, u32[]{:S(2)}) %collective-permute-start.3) | collective-permute-done | bytes 73760 | tf_op jit(solution)/shard_map/ppermute | solution.py:15
  25.0 4.3 %collective-permute-done.1 = f32[10,4,1,512]{3,2,1,0:T(1,128)S(1)} collective-permute-done((f32[10,4,1,512]{3,2,1,0:T(1,128)S(1)}, f32[10,4,1,512]{3,2,1,0:T(1,128)S(1)}, u32[]{:S(2)}, u32[]{:S(2)}) %collective-permute-start.1) | collective-permute-done | bytes 81952 | tf_op jit(solution)/shard_map/ppermute | solution.py:15
  29.9 86.6 %all-gather.2.cloned.1.call-done = f32[48,3,4,10,512]{4,2,3,1,0:T(4,128)} async-done(((f32[3,3,4,10,512]{4,2,3,1,0:T(4,128)}), f32[48,3,4,10,512]{4,2,3,1,0:T(4,128)}) %all-gather.2.cloned.1.call-update) | async-done | bytes 11796496 | tf_op jit(solution)/shard_map/all_gather | solution.py:98
  116.5 17.0 %copy.13 = f32[48,3,4,10,512]{4,3,2,1,0:T(8,128)} copy(f32[48,3,4,10,512]{4,2,3,1,0:T(4,128)} %all-gather.2.cloned.1.call-done) | data formatting | bytes 23592960 | tf_op jit(solution)/shard_map/while | solution.py:120
  133.5 281.4 %while.15 = (s32[]{:T(128)}, f32[3,3,4,8,512]{4,3,2,1,0:T(8,128)S(1)}, f32[3,48,9]{2,1,0:T(8,128)S(1)}, f32[9,4,10,512]{3,2,1,0:T(8,128)S(1)}, f32[48,3,4,10,512...) while((s32[]{:T(128)}, ...), condition=%wide.region_4.5_spmd, body=%wide.region_0.4_spmd.sunk | while | flops 4816939 | bytes 9204332 | solution.py:120
  134.9 3.1 conditional.2
  157.0 3.1 conditional.2
  173.3 3.1 conditional.2
  188.1 3.1 conditional.2
  194.1 3.1 conditional.2
  198.5 3.1 conditional.2
  211.9 3.1 conditional.2
  217.8 3.1 conditional.2
  231.2 3.1 conditional.2
  240.1 3.1 conditional.2
  265.2 3.1 conditional.2
  272.7 3.1 conditional.2
  303.7 3.1 conditional.2
  309.6 3.1 conditional.2
  333.4 3.1 conditional.2
  361.5 3.1 conditional.2
  395.5 3.1 conditional.2
  408.8 3.1 conditional.2
  (973 shorter events, 204.2 us)
Async XLA Ops:
  6.5 109.9 %all-gather.2.cloned.1.call-start = ((), (), s32[]{:S(2)}) async-start(), calls=%async_computation | async-start | bytes 12533760 | tf_op jit(solution)/shard_map/all_gather | solution.py:98
  8.0 12.5 %copy-start.5 = (f32[4,9]{1,0:T(4,128)S(1)}, f32[4,9]{1,0:T(4,128)}, u32[]{:S(2)}) copy-start(f32[4,9]{1,0:T(4,128)} %param.13) | copy-start | bytes 436
  8.0 12.5 %copy-start.3 = (s32[4,8,512]{2,1,0:T(8,128)S(1)}, s32[4,8,512]{2,1,0:T(8,128)}, u32[]{:S(2)}) copy-start(s32[4,8,512]{2,1,0:T(8,128)} %param.12) | copy-start | bytes 196612
  8.0 12.5 %copy-start.1 = (f32[9,4,8,512]{3,2,1,0:T(8,128)S(1)}, f32[9,4,8,512]{3,2,1,0:T(8,128)}, u32[]{:S(2)}) copy-start(f32[9,4,8,512]{3,2,1,0:T(8,128)} %param.11) | copy-start | bytes 1769476
  8.0 7.0 %collective-permute-start.2 = (f32[3,3,4,1,512]{4,2,3,1,0:T(4,128)S(1)}, f32[3,3,4,1,512]{4,2,3,1,0:T(4,128)S(1)}, u32[]{:S(2)}, u32[]{:S(2)}) collective-permute-start(f32[3,3,4,1,512]{4,2,3,1,0:T(4,128)S(1)} %get-tuple-element.391), channel_id=1, source_target_pairs={{0,16},{1,17},{2,18},{3,19},{4,20},{5,21},{6,22},{7,23},{8,24},{9,... | collective-permute-start | bytes 221192 | tf_op jit(solution)/shard_map/ppermute | solution.py:14
  13.1 6.2 %collective-permute-start.3 = (f32[3,3,4,1,512]{4,2,3,1,0:T(4,128)S(1)}, f32[3,3,4,1,512]{4,2,3,1,0:T(4,128)S(1)}, u32[]{:S(2)}, u32[]{:S(2)}) collective-permute-start(f32[3,3,4,1,512]{4,2,3,1,0:T(4,128)S(1)} %get-tuple-element.392), channel_id=1, source_target_pairs={{16,0},{17,1},{18,2},{19,3},{20,4},{21,5},{22,6},{23,7},{24,8},{25... | collective-permute-start | bytes 221192 | tf_op jit(solution)/shard_map/ppermute | solution.py:15
  20.4 0.8 copy-start.2
  20.5 3.8 copy-start.4
  20.5 3.8 copy-start.6
  21.4 3.6 collective-permute-start
  22.9 6.3 %collective-permute-start.1 = (f32[10,4,1,512]{3,2,1,0:T(1,128)S(1)}, f32[10,4,1,512]{3,2,1,0:T(1,128)S(1)}, u32[]{:S(2)}, u32[]{:S(2)}) collective-permute-start(f32[10,4,1,512]{3,2,1,0:T(1,128)S(1)} %get-tuple-element.390), channel_id=1, source_target_pairs={{16,0},{17,1},{18,2},{19,3},{20,4},{21,5},{22,6},{23,7},{24,8},{25... | collective-permute-start | bytes 245768 | tf_op jit(solution)/shard_map/ppermute | solution.py:15
  414.9 0.8 copy-start
Sparse Core Ops, SparseCore 0:
  20.6 95.8 all-gather.1
where the time goes:
time: 425 us; the launch traced here: 423 us
  other arithmetic  114 us (27%)
  loops' own time  107 us (25%)
  waiting for transfers between devices  96.2 us (23%)
  local copies, waits for them, and re-layouts  55.7 us (13%)
  matrix products  26.4 us (6%)
  between operations  13.6 us (3%)
  starting transfers between devices  9.18 us (2%)
    another operation x1, loops' own time, shards(): return lax.fori_loop(0, term_dev * block_terms, one_pair, zeros_out)  102 us
    reduce_or x144, other arithmetic, one_pair(): update = lax.cond(jnp.any(pair_weights != 0.0), apply_pair, skip_pair, 0)  96.1 us
    all_gather x1, waiting for transfers between devices, shards(): term_block = lax.all_gather(own_pad, 'chaos', axis=0, tiled=True)  86.6 us
    dot_general x23, matrix products, apply_pair(): jnp.einsum('k,kprc->prc', pair_weights, coef_pad, precision=lax.Precision...  26.2 us
    squeeze x23, local copies, waits for them, and re-layouts, apply_pair(): fields[1]  24.5 us
    while x2, local copies, waits for them, and re-layouts, shards(): return lax.fori_loop(0, term_dev * block_terms, one_pair, zeros_out)  17.1 us
    another operation x92, other arithmetic, jacobian_block(): return jnp.stack([out_potential, out_electron, out_holes], axis=-4)  11.4 us
    ppermute x2, waiting for transfers between devices, extended(): after = lax.ppermute(initial, axis, down)  8.58 us
  transfers between devices with their start and end apart: 5, of which 5 were waited for; matrix products, arithmetic and copies ran while one was open for 0% of the time, Pallas kernels for 0%

commit v1 on v0

--- a/solution.py
+++ b/solution.py
@@ -2,6 +2,16 @@
 import jax.numpy as jnp
 from jax import lax
 from jax.sharding import PartitionSpec as P
+
+
+def around_the_ring(array, axis, dim):
+    devices = lax.axis_size(axis)
+    block, blocks = (array, [array])
+    for _ in range(devices - 1):
+        block = lax.ppermute(block, axis, [(i, (i + 1) % devices) for i in range(devices)])
+        blocks.insert(0, block)
+    line = jnp.concatenate(blocks, axis=dim)
+    return jnp.roll(line, (lax.axis_index(axis) + 1) * array.shape[dim], axis=dim)
 
 
 def extended(array, sides, width):
@@ -95,7 +105,7 @@
     )
     zeros_out = jnp.zeros(direction.shape, jnp.float32)
     own_pad = extended(direction, (("space", 3),), 1)
-    term_block = lax.all_gather(own_pad, "chaos", axis=0, tiled=True)
+    term_block = around_the_ring(own_pad, "chaos", 0)
     block_terms = term_block.shape[0]
 
     def one_pair(pair_index, total):

time: 425 us -> 538 us (1.27)
  waiting for transfers between devices: 96.2 us -> 198 us
  local copies, waits for them, and re-layouts: 55.7 us -> 89.4 us
  between operations: 13.6 us -> 0.58 us
  loops' own time: 107 us -> 96.5 us
    ppermute x0 -> x15, waiting for transfers between devices: none -> 193 us  [around_the_ring(): lax.ppermute(block, axis, [(i, (i + 1) % devices) for i in range(devices)])]
    all_gather x1 -> x0, waiting for transfers between devices: 86.6 us -> none  [shards(): term_block = lax.all_gather(own_pad, 'chaos', axis=0, tiled=True)]
    unnamed x15 -> x78, local copies, waits for them, and re-layouts: 2.72 us -> 29 us
    another operation x1, loops' own time: 102 us -> 91.9 us  [shards(): return lax.fori_loop(0, term_dev * block_terms, one_pair, zeros_out)]
    dynamic_slice x0 -> x1, local copies, waits for them, and re-layouts: none -> 5.84 us  [around_the_ring(): jnp.roll(line, (lax.axis_index(axis) + 1) * array.shape[dim], axis=dim)]
  transfers between devices with their start and end apart: 5 -> 19, of which waited for: 5 -> 17; matrix products, arithmetic and copies ran while one was open for 0% -> 2% of each run, Pallas kernels for 0% -> 0%
where the time goes in v1:
time: 538 us; the launch traced here: 535 us
  waiting for transfers between devices  198 us (37%)
  other arithmetic  115 us (21%)
  loops' own time  96.5 us (18%)
  local copies, waits for them, and re-layouts  89.4 us (17%)
  matrix products  26.4 us (5%)
  starting transfers between devices  9.15 us (2%)
    ppermute x15, waiting for transfers between devices, around_the_ring(): lax.ppermute(block, axis, [(i, (i + 1) % devices) for i in range(devices)])  193 us
    reduce_or x144, other arithmetic, one_pair(): update = lax.cond(jnp.any(pair_weights != 0.0), apply_pair, skip_pair, 0)  91.9 us
    another operation x1, loops' own time, shards(): return lax.fori_loop(0, term_dev * block_terms, one_pair, zeros_out)  91.9 us
    unnamed x78, local copies, waits for them, and re-layouts  29 us
    dot_general x23, matrix products, apply_pair(): jnp.einsum('k,kprc->prc', pair_weights, coef_pad, precision=lax.Precision...  26.2 us
    squeeze x23, local copies, waits for them, and re-layouts, apply_pair(): fields[1]  24.5 us
    while x2, local copies, waits for them, and re-layouts, shards(): return lax.fori_loop(0, term_dev * block_terms, one_pair, zeros_out)  17.1 us
    another operation x92, other arithmetic, jacobian_block(): return jnp.stack([out_potential, out_electron, out_holes], axis=-4)  11.4 us
  transfers between devices with their start and end apart: 19, of which 17 were waited for; matrix products, arithmetic and copies ran while one was open for 2% of the time, Pallas kernels for 0%

profile of v1, /device:TPU:0, one launch (start us, length us, event | category | flops | bytes accessed | tf_op | source)
XLA Modules:
  0.0 534.9 jit_solution(3338871598042309790)
XLA Ops:
  1.5 4.9 collective-permute-start.2
  8.4 4.3 collective-permute-done.3
  13.0 13.6 %collective-permute-done.4 = f32[3,3,4,10,512]{4,2,3,1,0:T(4,128)S(1)} collective-permute-done((f32[3,3,4,10,512]{4,2,3,1,0:T(4,128)S(1)}, f32[3,3,4,10,512]{4,2,3,1,0:T(4,128)S(1)}, u32[]{:S(2)}, u32[]{:S(2)}) %collective-permute-start.4) | collective-permute-done | bytes 737312 | tf_op jit(solution)/shard_map/ppermute | solution.py:11
  26.5 13.6 %collective-permute-done.5 = f32[3,3,4,10,512]{4,2,3,1,0:T(4,128)S(1)} collective-permute-done((f32[3,3,4,10,512]{4,2,3,1,0:T(4,128)S(1)}, f32[3,3,4,10,512]{4,2,3,1,0:T(4,128)S(1)}, u32[]{:S(2)}, u32[]{:S(2)}) %collective-permute-start.5) | collective-permute-done | bytes 737312 | tf_op jit(solution)/shard_map/ppermute | solution.py:11
  40.1 13.6 %collective-permute-done.6 = f32[3,3,4,10,512]{4,2,3,1,0:T(4,128)S(1)} collective-permute-done((f32[3,3,4,10,512]{4,2,3,1,0:T(4,128)S(1)}, f32[3,3,4,10,512]{4,2,3,1,0:T(4,128)S(1)}, u32[]{:S(2)}, u32[]{:S(2)}) %collective-permute-start.6) | collective-permute-done | bytes 737312 | tf_op jit(solution)/shard_map/ppermute | solution.py:11
  54.6 13.6 %collective-permute-done.7 = f32[3,3,4,10,512]{4,2,3,1,0:T(4,128)S(1)} collective-permute-done((f32[3,3,4,10,512]{4,2,3,1,0:T(4,128)S(1)}, f32[3,3,4,10,512]{4,2,3,1,0:T(4,128)S(1)}, u32[]{:S(2)}, u32[]{:S(2)}) %collective-permute-start.7) | collective-permute-done | bytes 737312 | tf_op jit(solution)/shard_map/ppermute | solution.py:11
  69.1 13.6 %collective-permute-done.8 = f32[3,3,4,10,512]{4,2,3,1,0:T(4,128)S(1)} collective-permute-done((f32[3,3,4,10,512]{4,2,3,1,0:T(4,128)S(1)}, f32[3,3,4,10,512]{4,2,3,1,0:T(4,128)S(1)}, u32[]{:S(2)}, u32[]{:S(2)}) %collective-permute-start.8) | collective-permute-done | bytes 737312 | tf_op jit(solution)/shard_map/ppermute | solution.py:11
  82.7 13.6 %collective-permute-done.9 = f32[3,3,4,10,512]{4,2,3,1,0:T(4,128)S(1)} collective-permute-done((f32[3,3,4,10,512]{4,2,3,1,0:T(4,128)S(1)}, f32[3,3,4,10,512]{4,2,3,1,0:T(4,128)S(1)}, u32[]{:S(2)}, u32[]{:S(2)}) %collective-permute-start.9) | collective-permute-done | bytes 737312 | tf_op jit(solution)/shard_map/ppermute | solution.py:11
  97.1 13.6 %collective-permute-done.10 = f32[3,3,4,10,512]{4,2,3,1,0:T(4,128)S(1)} collective-permute-done((f32[3,3,4,10,512]{4,2,3,1,0:T(4,128)S(1)}, f32[3,3,4,10,512]{4,2,3,1,0:T(4,128)S(1)}, u32[]{:S(2)}, u32[]{:S(2)}) %collective-permute-start.10) | collective-permute-done | bytes 737312 | tf_op jit(solution)/shard_map/ppermute | solution.py:11
  111.6 13.6 %collective-permute-done.11 = f32[3,3,4,10,512]{4,2,3,1,0:T(4,128)S(1)} collective-permute-done((f32[3,3,4,10,512]{4,2,3,1,0:T(4,128)S(1)}, f32[3,3,4,10,512]{4,2,3,1,0:T(4,128)S(1)}, u32[]{:S(2)}, u32[]{:S(2)}) %collective-permute-start.11) | collective-permute-done | bytes 737312 | tf_op jit(solution)/shard_map/ppermute | solution.py:11
  126.0 13.6 %collective-permute-done.12 = f32[3,3,4,10,512]{4,2,3,1,0:T(4,128)S(1)} collective-permute-done((f32[3,3,4,10,512]{4,2,3,1,0:T(4,128)S(1)}, f32[3,3,4,10,512]{4,2,3,1,0:T(4,128)S(1)}, u32[]{:S(2)}, u32[]{:S(2)}) %collective-permute-start.12) | collective-permute-done | bytes 737312 | tf_op jit(solution)/shard_map/ppermute | solution.py:11
  140.5 13.6 %collective-permute-done.13 = f32[3,3,4,10,512]{4,2,3,1,0:T(4,128)S(1)} collective-permute-done((f32[3,3,4,10,512]{4,2,3,1,0:T(4,128)S(1)}, f32[3,3,4,10,512]{4,2,3,1,0:T(4,128)S(1)}, u32[]{:S(2)}, u32[]{:S(2)}) %collective-permute-start.13) | collective-permute-done | bytes 737312 | tf_op jit(solution)/shard_map/ppermute | solution.py:11
  155.0 13.6 %collective-permute-done.14 = f32[3,3,4,10,512]{4,2,3,1,0:T(4,128)S(1)} collective-permute-done((f32[3,3,4,10,512]{4,2,3,1,0:T(4,128)S(1)}, f32[3,3,4,10,512]{4,2,3,1,0:T(4,128)S(1)}, u32[]{:S(2)}, u32[]{:S(2)}) %collective-permute-start.14) | collective-permute-done | bytes 737312 | tf_op jit(solution)/shard_map/ppermute | solution.py:11
  169.5 12.8 %collective-permute-done.15 = f32[3,3,4,10,512]{4,2,3,1,0:T(4,128)} collective-permute-done((f32[3,3,4,10,512]{4,2,3,1,0:T(4,128)S(1)}, f32[3,3,4,10,512]{4,2,3,1,0:T(4,128)}, u32[]{:S(2)}, u32[]{:S(2)}) %collective-permute-start.15) | collective-permute-done | bytes 737312 | tf_op jit(solution)/shard_map/ppermute | solution.py:11
  189.2 7.0 %collective-permute-done.16 = f32[3,3,4,10,512]{4,2,3,1,0:T(4,128)} collective-permute-done((f32[3,3,4,10,512]{4,2,3,1,0:T(4,128)}, f32[3,3,4,10,512]{4,2,3,1,0:T(4,128)}, u32[]{:S(2)}, u32[]{:S(2)}) %collective-permute-start.16) | collective-permute-done | bytes 737312 | tf_op jit(solution)/shard_map/ppermute | solution.py:11
  198.5 11.5 %collective-permute-done.17 = f32[3,3,4,10,512]{4,2,3,1,0:T(4,128)} collective-permute-done((f32[3,3,4,10,512]{4,2,3,1,0:T(4,128)}, f32[3,3,4,10,512]{4,2,3,1,0:T(4,128)}, u32[]{:S(2)}, u32[]{:S(2)}) %collective-permute-start.17) | collective-permute-done | bytes 737312 | tf_op jit(solution)/shard_map/ppermute | solution.py:11
  211.3 12.6 %collective-permute-done.18 = f32[3,3,4,10,512]{4,2,3,1,0:T(4,128)S(1)} collective-permute-done((f32[3,3,4,10,512]{4,2,3,1,0:T(4,128)}, f32[3,3,4,10,512]{4,2,3,1,0:T(4,128)S(1)}, u32[]{:S(2)}, u32[]{:S(2)}) %collective-permute-start.18) | collective-permute-done | bytes 737312 | tf_op jit(solution)/shard_map/ppermute | solution.py:11
  244.6 5.8 %constant_dynamic-slice_fusion.2 = f32[48,3,4,10,512]{4,2,3,1,0:T(4,128)} fusion(f32[96,3,4,10,512]{4,2,3,1,0:T(4,128)S(1)} %constant_dynamic-update-slice_fusion, s32[]{:T(128)S(6)} %select_n.74), kind=kLoop, calls=%fused_computation.135 | loop fusion | bytes 23592964 | tf_op jit(solution)/shard_map/jit(_roll_dynamic)/dynamic_slice | solution.py:14
  250.5 17.0 %copy.13 = f32[48,3,4,10,512]{4,3,2,1,0:T(8,128)} copy(f32[48,3,4,10,512]{4,2,3,1,0:T(4,128)} %constant_dynamic-slice_fusion.2) | data formatting | bytes 23592960 | tf_op jit(solution)/shard_map/while | solution.py:130
  267.5 266.6 %while.15 = (s32[]{:T(128)}, f32[3,3,4,8,512]{4,3,2,1,0:T(8,128)S(1)}, f32[3,48,9]{2,1,0:T(8,128)S(1)}, f32[9,4,10,512]{3,2,1,0:T(8,128)S(1)}, f32[48,3,4,10,512...) while((s32[]{:T(128)}, ...), condition=%wide.region_4.5_spmd, body=%wide.region_0.4_spmd.sunk | while | flops 4816939 | bytes 9204332 | solution.py:130
  268.7 3.1 conditional.2
  289.6 3.1 conditional.2
  360.0 3.1 conditional.2
  368.5 3.1 conditional.2
  (1065 shorter events, 275.0 us)
Async XLA Ops:
  0.0 237.6 %copy-start = (f32[3,3,4,8,512]{4,3,2,1,0:T(8,128)S(1)}, f32[3,3,4,8,512]{4,3,2,1,0:T(8,128)}, u32[]{:S(2)}) copy-start(f32[3,3,4,8,512]{4,3,2,1,0:T(8,128)} %param.17) | copy-start | bytes 1769476
  1.5 6.9 %collective-permute-start.2 = (f32[3,3,4,1,512]{4,2,3,1,0:T(4,128)S(1)}, f32[3,3,4,1,512]{4,2,3,1,0:T(4,128)S(1)}, u32[]{:S(2)}, u32[]{:S(2)}) collective-permute-start(f32[3,3,4,1,512]{4,2,3,1,0:T(4,128)S(1)} %get-tuple-element.391), channel_id=1, source_target_pairs={{0,16},{1,17},{2,18},{3,19},{4,20},{5,21},{6,22},{7,23},{8,24},{9,... | collective-permute-start | bytes 221192 | tf_op jit(solution)/shard_map/ppermute | solution.py:24
  6.5 6.2 %collective-permute-start.3 = (f32[3,3,4,1,512]{4,2,3,1,0:T(4,128)S(1)}, f32[3,3,4,1,512]{4,2,3,1,0:T(4,128)S(1)}, u32[]{:S(2)}, u32[]{:S(2)}) collective-permute-start(f32[3,3,4,1,512]{4,2,3,1,0:T(4,128)S(1)} %get-tuple-element.392), channel_id=1, source_target_pairs={{16,0},{17,1},{18,2},{19,3},{20,4},{21,5},{22,6},{23,7},{24,8},{25... | collective-permute-start | bytes 221192 | tf_op jit(solution)/shard_map/ppermute | solution.py:25
  12.9 13.6 %collective-permute-start.4 = (f32[3,3,4,10,512]{4,2,3,1,0:T(4,128)S(1)}, f32[3,3,4,10,512]{4,2,3,1,0:T(4,128)S(1)}, u32[]{:S(2)}, u32[]{:S(2)}) collective-permute-start(f32[3,3,4,10,512]{4,2,3,1,0:T(4,128)S(1)} %pad_maximum_fusion.2), channel_id=1, source_target_pairs={{0,1},{1,2},{2,3},{3,4},{4,5},{5,6},{6,7},{7,8},{8,9},{9,10},{10,1... | collective-permute-start | bytes 2211848 | tf_op jit(solution)/shard_map/ppermute | solution.py:11
  26.5 13.6 %collective-permute-start.5 = (f32[3,3,4,10,512]{4,2,3,1,0:T(4,128)S(1)}, f32[3,3,4,10,512]{4,2,3,1,0:T(4,128)S(1)}, u32[]{:S(2)}, u32[]{:S(2)}) collective-permute-start(f32[3,3,4,10,512]{4,2,3,1,0:T(4,128)S(1)} %collective-permute-done.4), channel_id=1, source_target_pairs={{0,1},{1,2},{2,3},{3,4},{4,5},{5,6},{6,7},{7,8},{8,9},{9,10},{10,1... | collective-permute-start | bytes 2211848 | tf_op jit(solution)/shard_map/ppermute | solution.py:11
  40.1 142.9 %copy-start.2 = (f32[3,3,4,10,512]{4,2,3,1,0:T(4,128)}, f32[3,3,4,10,512]{4,2,3,1,0:T(4,128)S(1)}, u32[]{:S(2)}) copy-start(f32[3,3,4,10,512]{4,2,3,1,0:T(4,128)S(1)} %collective-permute-done.5) | copy-start | bytes 2211844
  40.1 13.6 %collective-permute-start.6 = (f32[3,3,4,10,512]{4,2,3,1,0:T(4,128)S(1)}, f32[3,3,4,10,512]{4,2,3,1,0:T(4,128)S(1)}, u32[]{:S(2)}, u32[]{:S(2)}) collective-permute-start(f32[3,3,4,10,512]{4,2,3,1,0:T(4,128)S(1)} %collective-permute-done.5), channel_id=1, source_target_pairs={{0,1},{1,2},{2,3},{3,4},{4,5},{5,6},{6,7},{7,8},{8,9},{9,10},{10,1... | collective-permute-start | bytes 2211848 | tf_op jit(solution)/shard_map/ppermute | solution.py:11
  54.6 13.6 %collective-permute-start.7 = (f32[3,3,4,10,512]{4,2,3,1,0:T(4,128)S(1)}, f32[3,3,4,10,512]{4,2,3,1,0:T(4,128)S(1)}, u32[]{:S(2)}, u32[]{:S(2)}) collective-permute-start(f32[3,3,4,10,512]{4,2,3,1,0:T(4,128)S(1)} %collective-permute-done.6), channel_id=1, source_target_pairs={{0,1},{1,2},{2,3},{3,4},{4,5},{5,6},{6,7},{7,8},{8,9},{9,10},{10,1... | collective-permute-start | bytes 2211848 | tf_op jit(solution)/shard_map/ppermute | solution.py:11
  69.1 13.6 %collective-permute-start.8 = (f32[3,3,4,10,512]{4,2,3,1,0:T(4,128)S(1)}, f32[3,3,4,10,512]{4,2,3,1,0:T(4,128)S(1)}, u32[]{:S(2)}, u32[]{:S(2)}) collective-permute-start(f32[3,3,4,10,512]{4,2,3,1,0:T(4,128)S(1)} %collective-permute-done.7), channel_id=1, source_target_pairs={{0,1},{1,2},{2,3},{3,4},{4,5},{5,6},{6,7},{7,8},{8,9},{9,10},{10,1... | collective-permute-start | bytes 2211848 | tf_op jit(solution)/shard_map/ppermute | solution.py:11
  82.6 127.4 %copy-start.7 = (f32[3,3,4,10,512]{4,2,3,1,0:T(4,128)}, f32[3,3,4,10,512]{4,2,3,1,0:T(4,128)S(1)}, u32[]{:S(2)}) copy-start(f32[3,3,4,10,512]{4,2,3,1,0:T(4,128)S(1)} %collective-permute-done.8) | copy-start | bytes 2211844
  82.6 13.6 %collective-permute-start.9 = (f32[3,3,4,10,512]{4,2,3,1,0:T(4,128)S(1)}, f32[3,3,4,10,512]{4,2,3,1,0:T(4,128)S(1)}, u32[]{:S(2)}, u32[]{:S(2)}) collective-permute-start(f32[3,3,4,10,512]{4,2,3,1,0:T(4,128)S(1)} %collective-permute-done.8), channel_id=1, source_target_pairs={{0,1},{1,2},{2,3},{3,4},{4,5},{5,6},{6,7},{7,8},{8,9},{9,10},{10,1... | collective-permute-start | bytes 2211848 | tf_op jit(solution)/shard_map/ppermute | solution.py:11
  97.1 13.6 %collective-permute-start.10 = (f32[3,3,4,10,512]{4,2,3,1,0:T(4,128)S(1)}, f32[3,3,4,10,512]{4,2,3,1,0:T(4,128)S(1)}, u32[]{:S(2)}, u32[]{:S(2)}) collective-permute-start(f32[3,3,4,10,512]{4,2,3,1,0:T(4,128)S(1)} %collective-permute-done.9), channel_id=1, source_target_pairs={{0,1},{1,2},{2,3},{3,4},{4,5},{5,6},{6,7},{7,8},{8,9},{9,10},{10,1... | collective-permute-start | bytes 2211848 | tf_op jit(solution)/shard_map/ppermute | solution.py:11
  111.5 13.6 %collective-permute-start.11 = (f32[3,3,4,10,512]{4,2,3,1,0:T(4,128)S(1)}, f32[3,3,4,10,512]{4,2,3,1,0:T(4,128)S(1)}, u32[]{:S(2)}, u32[]{:S(2)}) collective-permute-start(f32[3,3,4,10,512]{4,2,3,1,0:T(4,128)S(1)} %collective-permute-done.10), channel_id=1, source_target_pairs={{0,1},{1,2},{2,3},{3,4},{4,5},{5,6},{6,7},{7,8},{8,9},{9,10},{10,1... | collective-permute-start | bytes 2211848 | tf_op jit(solution)/shard_map/ppermute | solution.py:11
  126.0 13.6 %collective-permute-start.12 = (f32[3,3,4,10,512]{4,2,3,1,0:T(4,128)S(1)}, f32[3,3,4,10,512]{4,2,3,1,0:T(4,128)S(1)}, u32[]{:S(2)}, u32[]{:S(2)}) collective-permute-start(f32[3,3,4,10,512]{4,2,3,1,0:T(4,128)S(1)} %collective-permute-done.11), channel_id=1, source_target_pairs={{0,1},{1,2},{2,3},{3,4},{4,5},{5,6},{6,7},{7,8},{8,9},{9,10},{10,1... | collective-permute-start | bytes 2211848 | tf_op jit(solution)/shard_map/ppermute | solution.py:11
  140.5 13.6 %collective-permute-start.13 = (f32[3,3,4,10,512]{4,2,3,1,0:T(4,128)S(1)}, f32[3,3,4,10,512]{4,2,3,1,0:T(4,128)S(1)}, u32[]{:S(2)}, u32[]{:S(2)}) collective-permute-start(f32[3,3,4,10,512]{4,2,3,1,0:T(4,128)S(1)} %collective-permute-done.12), channel_id=1, source_target_pairs={{0,1},{1,2},{2,3},{3,4},{4,5},{5,6},{6,7},{7,8},{8,9},{9,10},{10,1... | collective-permute-start | bytes 2211848 | tf_op jit(solution)/shard_map/ppermute | solution.py:11
  155.0 13.6 %collective-permute-start.14 = (f32[3,3,4,10,512]{4,2,3,1,0:T(4,128)S(1)}, f32[3,3,4,10,512]{4,2,3,1,0:T(4,128)S(1)}, u32[]{:S(2)}, u32[]{:S(2)}) collective-permute-start(f32[3,3,4,10,512]{4,2,3,1,0:T(4,128)S(1)} %collective-permute-done.13), channel_id=1, source_target_pairs={{0,1},{1,2},{2,3},{3,4},{4,5},{5,6},{6,7},{7,8},{8,9},{9,10},{10,1... | collective-permute-start | bytes 2211848 | tf_op jit(solution)/shard_map/ppermute | solution.py:11
  168.5 13.7 %collective-permute-start.15 = (f32[3,3,4,10,512]{4,2,3,1,0:T(4,128)S(1)}, f32[3,3,4,10,512]{4,2,3,1,0:T(4,128)}, u32[]{:S(2)}, u32[]{:S(2)}) collective-permute-start(f32[3,3,4,10,512]{4,2,3,1,0:T(4,128)S(1)} %collective-permute-done.14), channel_id=1, source_target_pairs={{0,1},{1,2},{2,3},{3,4},{4,5},{5,6},{6,7},{7,8},{8,9},{9,10},{10,1... | collective-permute-start | bytes 2211848 | tf_op jit(solution)/shard_map/ppermute | solution.py:11
  182.2 13.9 %collective-permute-start.16 = (f32[3,3,4,10,512]{4,2,3,1,0:T(4,128)}, f32[3,3,4,10,512]{4,2,3,1,0:T(4,128)}, u32[]{:S(2)}, u32[]{:S(2)}) collective-permute-start(f32[3,3,4,10,512]{4,2,3,1,0:T(4,128)} %collective-permute-done.15), channel_id=1, source_target_pairs={{0,1},{1,2},{2,3},{3,4},{4,5},{5,6},{6,7},{7,8},{8,9},{9,10},{10,1... | collective-permute-start | bytes 2211848 | tf_op jit(solution)/shard_map/ppermute | solution.py:11
  185.5 11.8 %collective-permute-start = (f32[10,4,1,512]{3,2,1,0:T(1,128)S(1)}, f32[10,4,1,512]{3,2,1,0:T(1,128)S(1)}, u32[]{:S(2)}, u32[]{:S(2)}) collective-permute-start(f32[10,4,1,512]{3,2,1,0:T(1,128)S(1)} %get-tuple-element.389), channel_id=1, source_target_pairs={{0,16},{1,17},{2,18},{3,19},{4,20},{5,21},{6,22},{7,23},{8,24},{9,... | collective-permute-start | bytes 245768 | tf_op jit(solution)/shard_map/ppermute | solution.py:24
  187.0 10.3 %collective-permute-start.1 = (f32[10,4,1,512]{3,2,1,0:T(1,128)S(1)}, f32[10,4,1,512]{3,2,1,0:T(1,128)S(1)}, u32[]{:S(2)}, u32[]{:S(2)}) collective-permute-start(f32[10,4,1,512]{3,2,1,0:T(1,128)S(1)} %get-tuple-element.390), channel_id=1, source_target_pairs={{16,0},{17,1},{18,2},{19,3},{20,4},{21,5},{22,6},{23,7},{24,8},{25... | collective-permute-start | bytes 245768 | tf_op jit(solution)/shard_map/ppermute | solution.py:25
  196.1 13.9 %collective-permute-start.17 = (f32[3,3,4,10,512]{4,2,3,1,0:T(4,128)}, f32[3,3,4,10,512]{4,2,3,1,0:T(4,128)}, u32[]{:S(2)}, u32[]{:S(2)}) collective-permute-start(f32[3,3,4,10,512]{4,2,3,1,0:T(4,128)} %collective-permute-done.16), channel_id=1, source_target_pairs={{0,1},{1,2},{2,3},{3,4},{4,5},{5,6},{6,7},{7,8},{8,9},{9,10},{10,1... | collective-permute-start | bytes 2211848 | tf_op jit(solution)/shard_map/ppermute | solution.py:11
  197.3 45.0 %copy-start.12 = (f32[3,3,4,10,512]{4,2,3,1,0:T(4,128)S(1)}, f32[3,3,4,10,512]{4,2,3,1,0:T(4,128)}, u32[]{:S(2)}) copy-start(f32[3,3,4,10,512]{4,2,3,1,0:T(4,128)} %copy-done.11) | copy-start | bytes 2211844
  197.3 45.1 %copy-start.10 = (f32[3,3,4,10,512]{4,2,3,1,0:T(4,128)S(1)}, f32[3,3,4,10,512]{4,2,3,1,0:T(4,128)}, u32[]{:S(2)}) copy-start(f32[3,3,4,10,512]{4,2,3,1,0:T(4,128)} %copy-done.9) | copy-start | bytes 2211844
  210.0 13.8 %collective-permute-start.18 = (f32[3,3,4,10,512]{4,2,3,1,0:T(4,128)}, f32[3,3,4,10,512]{4,2,3,1,0:T(4,128)S(1)}, u32[]{:S(2)}, u32[]{:S(2)}) collective-permute-start(f32[3,3,4,10,512]{4,2,3,1,0:T(4,128)} %collective-permute-done.17), channel_id=1, source_target_pairs={{0,1},{1,2},{2,3},{3,4},{4,5},{5,6},{6,7},{7,8},{8,9},{9,10},{10,1... | collective-permute-start | bytes 2211848 | tf_op jit(solution)/shard_map/ppermute | solution.py:11
  (16 other events, 312.3 us)
